TPU v7x, 32 devices: a whole 2x2x4 slice. The times are simulated.
32 devices in a mesh: rep: 2 (over x), ctx: 8 (over z, y), tp: 2 (over core).
Axes of the slice: x: 2, y: 2, z: 4, core: 2. Of those that a mesh axis runs over, the one named last changes fastest.
Arguments:
- queries: bfloat16 [4096, 4096], P(('rep', 'ctx'), 'tp'), parts along dimension 0, may hold values from -8 to 8
- rotated_key_rows: bfloat16 [4096, 512], P(('rep', 'ctx'), 'tp'), parts along dimension 0, may hold values from -8 to 8
- ordered_value_rows: bfloat16 [4096, 512], P(('rep', 'ctx'), 'tp'), parts along dimension 0, may hold values from -6 to 6
- block_order: int32 [32], P('rep'), parts along dimension 0, may hold values from 0 to 15, each once
- live_blocks: int32 [32, 12], P('rep'), parts along dimension 0, may hold values from -1 to 15, as said below
Outputs:
- attended: bfloat16 [4096, 4096], P(('rep', 'ctx', 'tp')), parts along dimension 0
- log_norm: float32 [64, 2048], P(('rep', 'tp'), 'ctx'), parts along dimension 0
There are 2 independent parts, one for each index of `rep`. A program takes and returns all parts, laid end to end along the dimension named above; each array names one. Nothing has to cross between parts.
Inputs may be any that keep to these rules, and one draw needn't show every extreme that they name: `live_blocks`: row s names block s in its first slot, then distinct blocks before s, then -1 in every unused slot; row 15 fills all 12 slots.
All inputs are finite; a program needn't handle non-finite values.
Results may differ from a plain program's by a relative error of at most 0.008.
Values may be sent and summed in bfloat16 or wider, within the bound.
A program may use at most 128 MiB of HBM per device.

v0:
```python
import jax
import jax.numpy as jnp
from jax import lax
from jax.sharding import PartitionSpec as P

HEAD_SIZE = 128
BLOCK_TOKENS = 128
NEG_LARGE = -1e30


def body(queries, rotated_key_rows, ordered_value_rows, block_order, live_blocks):
    tok_rows = queries.shape[0]
    kv_local = rotated_key_rows.shape[1] // HEAD_SIZE
    heads_local = queries.shape[1] // HEAD_SIZE
    query_groups = heads_local // kv_local
    blocks_total = block_order.shape[0]
    blocks_here = tok_rows // BLOCK_TOKENS
    factor = HEAD_SIZE ** (-0.5)
    shard_index = lax.axis_index("ctx")
    block_ids = jnp.arange(blocks_total, dtype=jnp.int32)
    my_blocks = lax.dynamic_slice_in_dim(block_order, shard_index * blocks_here, blocks_here)
    my_lists = jnp.take(live_blocks, my_blocks, axis=0)
    live_table = jnp.any(my_lists[:, :, None] == block_ids[None, None, :], axis=1)
    within = jnp.arange(BLOCK_TOKENS, dtype=jnp.int32)
    causal_square = within[None, :] <= within[:, None]
    query_heads = queries.reshape(tok_rows, kv_local, query_groups, HEAD_SIZE)
    carried = tuple(
        (
            (
                jnp.full((kv_local, query_groups, BLOCK_TOKENS), NEG_LARGE, jnp.float32),
                jnp.zeros((kv_local, query_groups, BLOCK_TOKENS), jnp.float32),
                jnp.zeros((kv_local, query_groups, BLOCK_TOKENS, HEAD_SIZE), jnp.float32),
            )
            for block_local in range(blocks_here)
        )
    )
    key_piece = lax.all_gather(rotated_key_rows, "ctx", axis=0, tiled=True)
    value_piece = lax.all_gather(ordered_value_rows, "ctx", axis=0, tiled=True)
    key_blocks = key_piece.shape[0] // BLOCK_TOKENS

    def one_key_block(turn_index, states):
        offset = turn_index * BLOCK_TOKENS
        key_part = lax.dynamic_slice_in_dim(key_piece, offset, BLOCK_TOKENS).reshape(
            BLOCK_TOKENS, kv_local, HEAD_SIZE
        )
        value_part = lax.dynamic_slice_in_dim(value_piece, offset, BLOCK_TOKENS).reshape(
            BLOCK_TOKENS, kv_local, HEAD_SIZE
        )
        key_seq = block_order[offset // BLOCK_TOKENS]
        updated = []
        for block_local in range(blocks_here):
            query_part = query_heads[block_local * BLOCK_TOKENS : (block_local + 1) * BLOCK_TOKENS]
            allowed = (key_seq != my_blocks[block_local]) | causal_square

            def compute_tile(current):
                running, denominator, weighted = current
                scores = (
                    jnp.einsum(
                        "qhgd,khd->hgqk", query_part, key_part, preferred_element_type=jnp.float32
                    )
                    * factor
                )
                scores = jnp.where(allowed, scores, NEG_LARGE)
                new_peak = jnp.maximum(running, jnp.max(scores, axis=-1))
                weights = jnp.where(allowed, jnp.exp(scores - new_peak[..., None]), 0.0)
                rescale = jnp.exp(running - new_peak)
                denominator = denominator * rescale + jnp.sum(weights, axis=-1)
                weighted = weighted * rescale[..., None] + jnp.einsum(
                    "hgqk,khd->hgqd",
                    weights.astype(jnp.bfloat16),
                    value_part,
                    preferred_element_type=jnp.float32,
                )
                return (new_peak, denominator, weighted)

            updated.append(
                lax.cond(
                    live_table[block_local, key_seq],
                    compute_tile,
                    lambda current: current,
                    states[block_local],
                )
            )
        return tuple(updated)

    states = lax.fori_loop(0, key_blocks, one_key_block, carried)
    running = jnp.concatenate([item[0] for item in states], axis=2)
    denominator = jnp.concatenate([item[1] for item in states], axis=2)
    weighted = jnp.concatenate([item[2] for item in states], axis=2)
    normed = weighted / denominator[..., None]
    merged_out = (
        jnp.transpose(normed, (2, 0, 1, 3))
        .reshape(tok_rows, heads_local * HEAD_SIZE)
        .astype(jnp.bfloat16)
    )
    log_norm = (running + jnp.log(denominator)).reshape(heads_local, tok_rows)
    attended = lax.all_to_all(merged_out, "tp", split_axis=0, concat_axis=1, tiled=True)
    return (attended, log_norm)


def solution(mesh):
    placed = (
        P(("rep", "ctx"), "tp"),
        P(("rep", "ctx"), "tp"),
        P(("rep", "ctx"), "tp"),
        P("rep"),
        P("rep", None),
    )
    return jax.shard_map(
        body,
        mesh=mesh,
        in_specs=placed,
        out_specs=(P(("rep", "ctx", "tp"), None), P(("rep", "tp"), "ctx")),
        check_vma=False,
    )
```

profile of v0, /device:TPU:0, one launch (start us, length us, event | category | flops | bytes accessed | tf_op | source)
XLA Modules:
  0.0 250.6 jit_solution(15988656583783142846)
XLA Ops:
  13.7 39.1 %all-gather.3.cloned.1.call-done = bf16[2048,256]{0,1:T(8,128)(2,1)} async-done(((bf16[256,256]{0,1:T(8,128)(2,1)}), bf16[2048,256]{0,1:T(8,128)(2,1)}) %all-gather.3.cloned.1.call-update) | async-done | bytes 1048592 | tf_op jit(solution)/shard_map/all_gather | solution.py:37
  52.8 40.5 %all-gather.5.cloned.1.call-done = bf16[2048,256]{0,1:T(8,128)(2,1)} async-done(((bf16[256,256]{0,1:T(8,128)(2,1)}), bf16[2048,256]{0,1:T(8,128)(2,1)}) %all-gather.5.cloned.1.call-update) | async-done | bytes 1048592 | tf_op jit(solution)/shard_map/all_gather | solution.py:38
  93.5 141.2 %while.27 = (s32[]{:T(128)}, f32[2,8,128]{2,1,0:T(8,128)S(1)}, f32[2,8,128]{2,1,0:T(8,128)S(1)}, f32[2,8,128,128]{3,2,1,0:T(8,128)S(1)}, f32[2,8,128]{2,1,0:T(8,...) while((s32[]{:T(128)}, f32[2,8,128]{2,1,0:T(8,128)S(1)}, ...), condition=%wide.region_10.11_spmd.clone.clone, body=%wide.region_1.10_spmd.clone.clone.sunk | while | flops 274260000 | bytes 12501754 | solution.py:86
  98.9 2.0 conditional.8
  106.3 3.3 %conditional.9 = ((f32[2,8,128]{2,1,0:T(8,128)S(1)}, f32[2,8,128]{2,1,0:T(8,128)S(1)}, f32[2,8,128,128]{3,2,1,0:T(8,128)S(1)})) conditional(s32[]{:T(128)} %bitcast.60, (f32[2,8,128]{2,1,0:T(8,128)S(1)}, f32[2,8,128]{2,1,0:T(8,128)S(1)}, f32[2,8,128,128]{3,2,1,0:T(8,128)S(1)}) %tuple.96, (s32[2]{0:T(128)S(1)}, s32[]{:T(128)}, ...), branch_computations={%region_6.6_spmd, %region_7.9_spmd} | conditional | flops 137121792 | bytes 6111282 | solution.py:77
  115.0 2.0 conditional.8
  117.1 3.3 %conditional.9 = ((f32[2,8,128]{2,1,0:T(8,128)S(1)}, f32[2,8,128]{2,1,0:T(8,128)S(1)}, f32[2,8,128,128]{3,2,1,0:T(8,128)S(1)})) conditional(s32[]{:T(128)} %bitcast.60, (f32[2,8,128]{2,1,0:T(8,128)S(1)}, f32[2,8,128]{2,1,0:T(8,128)S(1)}, f32[2,8,128,128]{3,2,1,0:T(8,128)S(1)}) %tuple.96, (s32[2]{0:T(128)S(1)}, s32[]{:T(128)}, ...), branch_computations={%region_6.6_spmd, %region_7.9_spmd} | conditional | flops 137121792 | bytes 6111282 | solution.py:77
  125.8 2.0 conditional.8
  127.8 3.3 %conditional.9 = ((f32[2,8,128]{2,1,0:T(8,128)S(1)}, f32[2,8,128]{2,1,0:T(8,128)S(1)}, f32[2,8,128,128]{3,2,1,0:T(8,128)S(1)})) conditional(s32[]{:T(128)} %bitcast.60, (f32[2,8,128]{2,1,0:T(8,128)S(1)}, f32[2,8,128]{2,1,0:T(8,128)S(1)}, f32[2,8,128,128]{3,2,1,0:T(8,128)S(1)}) %tuple.96, (s32[2]{0:T(128)S(1)}, s32[]{:T(128)}, ...), branch_computations={%region_6.6_spmd, %region_7.9_spmd} | conditional | flops 137121792 | bytes 6111282 | solution.py:77
  136.5 2.0 conditional.8
  138.5 3.3 %conditional.9 = ((f32[2,8,128]{2,1,0:T(8,128)S(1)}, f32[2,8,128]{2,1,0:T(8,128)S(1)}, f32[2,8,128,128]{3,2,1,0:T(8,128)S(1)})) conditional(s32[]{:T(128)} %bitcast.60, (f32[2,8,128]{2,1,0:T(8,128)S(1)}, f32[2,8,128]{2,1,0:T(8,128)S(1)}, f32[2,8,128,128]{3,2,1,0:T(8,128)S(1)}) %tuple.96, (s32[2]{0:T(128)S(1)}, s32[]{:T(128)}, ...), branch_computations={%region_6.6_spmd, %region_7.9_spmd} | conditional | flops 137121792 | bytes 6111282 | solution.py:77
  147.2 2.0 conditional.8
  149.2 3.3 %conditional.9 = ((f32[2,8,128]{2,1,0:T(8,128)S(1)}, f32[2,8,128]{2,1,0:T(8,128)S(1)}, f32[2,8,128,128]{3,2,1,0:T(8,128)S(1)})) conditional(s32[]{:T(128)} %bitcast.60, (f32[2,8,128]{2,1,0:T(8,128)S(1)}, f32[2,8,128]{2,1,0:T(8,128)S(1)}, f32[2,8,128,128]{3,2,1,0:T(8,128)S(1)}) %tuple.96, (s32[2]{0:T(128)S(1)}, s32[]{:T(128)}, ...), branch_computations={%region_6.6_spmd, %region_7.9_spmd} | conditional | flops 137121792 | bytes 6111282 | solution.py:77
  163.4 3.3 %conditional.9 = ((f32[2,8,128]{2,1,0:T(8,128)S(1)}, f32[2,8,128]{2,1,0:T(8,128)S(1)}, f32[2,8,128,128]{3,2,1,0:T(8,128)S(1)})) conditional(s32[]{:T(128)} %bitcast.60, (f32[2,8,128]{2,1,0:T(8,128)S(1)}, f32[2,8,128]{2,1,0:T(8,128)S(1)}, f32[2,8,128,128]{3,2,1,0:T(8,128)S(1)}) %tuple.96, (s32[2]{0:T(128)S(1)}, s32[]{:T(128)}, ...), branch_computations={%region_6.6_spmd, %region_7.9_spmd} | conditional | flops 137121792 | bytes 6111282 | solution.py:77
  172.1 3.3 %conditional.9 = ((f32[2,8,128]{2,1,0:T(8,128)S(1)}, f32[2,8,128]{2,1,0:T(8,128)S(1)}, f32[2,8,128,128]{3,2,1,0:T(8,128)S(1)})) conditional(s32[]{:T(128)} %bitcast.60, (f32[2,8,128]{2,1,0:T(8,128)S(1)}, f32[2,8,128]{2,1,0:T(8,128)S(1)}, f32[2,8,128,128]{3,2,1,0:T(8,128)S(1)}) %tuple.96, (s32[2]{0:T(128)S(1)}, s32[]{:T(128)}, ...), branch_computations={%region_6.6_spmd, %region_7.9_spmd} | conditional | flops 137121792 | bytes 6111282 | solution.py:77
  180.8 2.0 conditional.8
  182.8 3.3 %conditional.9 = ((f32[2,8,128]{2,1,0:T(8,128)S(1)}, f32[2,8,128]{2,1,0:T(8,128)S(1)}, f32[2,8,128,128]{3,2,1,0:T(8,128)S(1)})) conditional(s32[]{:T(128)} %bitcast.60, (f32[2,8,128]{2,1,0:T(8,128)S(1)}, f32[2,8,128]{2,1,0:T(8,128)S(1)}, f32[2,8,128,128]{3,2,1,0:T(8,128)S(1)}) %tuple.96, (s32[2]{0:T(128)S(1)}, s32[]{:T(128)}, ...), branch_computations={%region_6.6_spmd, %region_7.9_spmd} | conditional | flops 137121792 | bytes 6111282 | solution.py:77
  191.5 2.0 conditional.8
  193.5 3.3 %conditional.9 = ((f32[2,8,128]{2,1,0:T(8,128)S(1)}, f32[2,8,128]{2,1,0:T(8,128)S(1)}, f32[2,8,128,128]{3,2,1,0:T(8,128)S(1)})) conditional(s32[]{:T(128)} %bitcast.60, (f32[2,8,128]{2,1,0:T(8,128)S(1)}, f32[2,8,128]{2,1,0:T(8,128)S(1)}, f32[2,8,128,128]{3,2,1,0:T(8,128)S(1)}) %tuple.96, (s32[2]{0:T(128)S(1)}, s32[]{:T(128)}, ...), branch_computations={%region_6.6_spmd, %region_7.9_spmd} | conditional | flops 137121792 | bytes 6111282 | solution.py:77
  207.7 3.3 %conditional.9 = ((f32[2,8,128]{2,1,0:T(8,128)S(1)}, f32[2,8,128]{2,1,0:T(8,128)S(1)}, f32[2,8,128,128]{3,2,1,0:T(8,128)S(1)})) conditional(s32[]{:T(128)} %bitcast.60, (f32[2,8,128]{2,1,0:T(8,128)S(1)}, f32[2,8,128]{2,1,0:T(8,128)S(1)}, f32[2,8,128,128]{3,2,1,0:T(8,128)S(1)}) %tuple.96, (s32[2]{0:T(128)S(1)}, s32[]{:T(128)}, ...), branch_computations={%region_6.6_spmd, %region_7.9_spmd} | conditional | flops 137121792 | bytes 6111282 | solution.py:77
  221.9 2.0 conditional.8
  229.4 2.0 conditional.8
  231.4 3.3 %conditional.9 = ((f32[2,8,128]{2,1,0:T(8,128)S(1)}, f32[2,8,128]{2,1,0:T(8,128)S(1)}, f32[2,8,128,128]{3,2,1,0:T(8,128)S(1)})) conditional(s32[]{:T(128)} %bitcast.60, (f32[2,8,128]{2,1,0:T(8,128)S(1)}, f32[2,8,128]{2,1,0:T(8,128)S(1)}, f32[2,8,128,128]{3,2,1,0:T(8,128)S(1)}) %tuple.96, (s32[2]{0:T(128)S(1)}, s32[]{:T(128)}, ...), branch_computations={%region_6.6_spmd, %region_7.9_spmd} | conditional | flops 137121792 | bytes 6111282 | solution.py:77
  236.6 4.6 %all_to_all.16 = bf16[2,128,2048]{2,1,0:T(8,128)(2,1)S(1)} all-to-all(bf16[2,128,2048]{2,1,0:T(8,128)(2,1)S(1)} %convert_element_type.44), channel_id=1, replica_groups=mesh['rep'=2,'ctx'=8,'tp'=2] {'tp'}, dimensions={0} | all-to-all | bytes 2097152 | tf_op jit(solution)/shard_map/all_to_all | solution.py:97
  (258 shorter events, 78.4 us)
Async XLA Ops:
  7.2 5.8 %copy-start = (s32[16,12]{1,0:T(8,128)S(1)}, s32[16,12]{1,0:T(8,128)}, u32[]{:S(2)}) copy-start(s32[16,12]{1,0:T(8,128)} %param.15) | copy-start | bytes 2308
  7.2 45.6 %all-gather.3.cloned.1.call-start = ((), (), s32[]{:S(2)}) async-start(), calls=%async_computation.1 | async-start | bytes 1179648 | tf_op jit(solution)/shard_map/all_gather | solution.py:37
  8.9 84.3 %all-gather.5.cloned.1.call-start = ((), (), s32[]{:S(2)}) async-start(), calls=%async_computation.2 | async-start | bytes 1179648 | tf_op jit(solution)/shard_map/all_gather | solution.py:38
  12.1 0.7 copy-start.1
Sparse Core Ops, SparseCore 0:
  10.6 42.1 all-gather.2
  54.8 38.3 all-gather.4
where the time goes:
time: 253 us; the launch traced here: 251 us
  waiting for transfers between devices  79.6 us (31%)
  loops' own time  74.1 us (29%)
  local copies, waits for them, and re-layouts  50.8 us (20%)
  matrix products  21 us (8%)
  between operations  14.2 us (6%)
  other arithmetic  6.35 us (3%)
  blocking collectives  4.58 us (2%)
    another operation x1, loops' own time, body(): states = lax.fori_loop(0, key_blocks, one_key_block, carried)  52.4 us
    all_gather x1, waiting for transfers between devices, body(): value_piece = lax.all_gather(ordered_value_rows, 'ctx', axis=0, tiled=True)  40.5 us
    all_gather x1, waiting for transfers between devices, body(): key_piece = lax.all_gather(rotated_key_rows, 'ctx', axis=0, tiled=True)  39.1 us
    another operation x32, loops' own time, one_key_block(): lax.cond(live_table[block_local, key_seq], compute_tile, lambda current:...  21.7 us
    dynamic_slice x16, local copies, waits for them, and re-layouts, one_key_block(): lax.dynamic_slice_in_dim(value_piece, offset, BLOCK_TOKENS)  14.3 us
    dot_general x20, matrix products, compute_tile(): jnp.einsum('hgqk,khd->hgqd', weights.astype(jnp.bfloat16), value_part, pr...  13.7 us
    dynamic_slice x16, local copies, waits for them, and re-layouts, one_key_block(): live_table[block_local, key_seq]  10.6 us
    dynamic_slice x16, local copies, waits for them, and re-layouts, one_key_block(): key_seq = block_order[offset // BLOCK_TOKENS]  9.39 us
  transfers between devices with their start and end apart: 2, of which 2 were waited for; matrix products, arithmetic and copies ran while one was open for 2% of the time, Pallas kernels for 0%

commit v1 on v0

--- a/solution.py
+++ b/solution.py
@@ -9,6 +9,32 @@
 
 
 def body(queries, rotated_key_rows, ordered_value_rows, block_order, live_blocks):
+
+    def search_the_meshes(vec):
+        oldest, y2, main = (lax.axis_size("ctx"), lax.axis_index("ctx"), vec.shape[0])
+        p_next = lax.dynamic_update_slice_in_dim(
+            jnp.zeros([s * oldest if pp == 0 else s for pp, s in enumerate(vec.shape)], vec.dtype),
+            vec,
+            y2 * main,
+            axis=0,
+        )
+        wide_out = x_next = vec
+        for nth in range(1, oldest // 2 + 1):
+            wide_out = lax.ppermute(
+                wide_out, "ctx", [(pp, (pp + 1) % oldest) for pp in range(oldest)]
+            )
+            p_next = lax.dynamic_update_slice_in_dim(
+                p_next, wide_out, (y2 - nth) % oldest * main, axis=0
+            )
+            if 2 * nth < oldest:
+                x_next = lax.ppermute(
+                    x_next, "ctx", [(pp, (pp - 1) % oldest) for pp in range(oldest)]
+                )
+                p_next = lax.dynamic_update_slice_in_dim(
+                    p_next, x_next, (y2 + nth) % oldest * main, axis=0
+                )
+        return p_next
+
     tok_rows = queries.shape[0]
     kv_local = rotated_key_rows.shape[1] // HEAD_SIZE
     heads_local = queries.shape[1] // HEAD_SIZE
@@ -35,7 +61,7 @@
         )
     )
     key_piece = lax.all_gather(rotated_key_rows, "ctx", axis=0, tiled=True)
-    value_piece = lax.all_gather(ordered_value_rows, "ctx", axis=0, tiled=True)
+    value_piece = search_the_meshes(ordered_value_rows)
     key_blocks = key_piece.shape[0] // BLOCK_TOKENS
 
     def one_key_block(turn_index, states):

time: 253 us -> 211 us (0.83)
  waiting for transfers between devices: 79.6 us -> 21.8 us
  starting transfers between devices: 0.08 us -> 16.2 us
  loops' own time: 74.1 us -> 68 us
  local copies, waits for them, and re-layouts: 50.8 us -> 56.2 us
    all_gather x1 -> x0, waiting for transfers between devices: 40.5 us -> none  [body(): value_piece = lax.all_gather(ordered_value_rows, 'ctx', axis=0, tiled=True)]
    all_gather x1, waiting for transfers between devices: 39.1 us -> 4.22 us  [body(): key_piece = lax.all_gather(rotated_key_rows, 'ctx', axis=0, tiled=True)]
    ppermute x0 -> x7, waiting for transfers between devices: none -> 17.6 us  [the longest x4 15.3 us: search_the_meshes(): lax.ppermute(wide_out, 'ctx', [(pp, (pp + 1) % oldest) for pp in range(ol...]
    ppermute x0 -> x7, starting transfers between devices: none -> 16.2 us  [the longest x3 16.2 us: search_the_meshes(): lax.ppermute(x_next, 'ctx', [(pp, (pp - 1) % oldest) for pp in range(olde...]
    dynamic_update_slice x0 -> x8, local copies, waits for them, and re-layouts: none -> 5.31 us  [the longest x4 2.66 us: search_the_meshes(): lax.dynamic_update_slice_in_dim(p_next, wide_out, (y2 - nth) % oldest * m...]
    another operation x1, loops' own time: 52.4 us -> 48.6 us  [body(): states = lax.fori_loop(0, key_blocks, one_key_block, carried)]
  transfers between devices with their start and end apart: 2 -> 8, of which waited for: 2 -> 4; matrix products, arithmetic and copies ran while one was open for 2% -> 5% of each run, Pallas kernels for 0% -> 0%
where the time goes in v1:
time: 211 us; the launch traced here: 209 us
  loops' own time  68 us (32%)
  local copies, waits for them, and re-layouts  56.2 us (27%)
  waiting for transfers between devices  21.8 us (10%)
  matrix products  21 us (10%)
  starting transfers between devices  16.2 us (8%)
  between operations  14.3 us (7%)
  other arithmetic  6.99 us (3%)
  blocking collectives  4.58 us (2%)
    another operation x1, loops' own time, body(): states = lax.fori_loop(0, key_blocks, one_key_block, carried)  48.6 us
    another operation x32, loops' own time, one_key_block(): lax.cond(live_table[block_local, key_seq], compute_tile, lambda current:...  19.3 us
    ppermute x3, starting transfers between devices, search_the_meshes(): lax.ppermute(x_next, 'ctx', [(pp, (pp - 1) % oldest) for pp in range(olde...  16.2 us
    ppermute x4, waiting for transfers between devices, search_the_meshes(): lax.ppermute(wide_out, 'ctx', [(pp, (pp + 1) % oldest) for pp in range(ol...  15.3 us
    dynamic_slice x16, local copies, waits for them, and re-layouts, one_key_block(): lax.dynamic_slice_in_dim(value_piece, offset, BLOCK_TOKENS)  14.2 us
    dot_general x20, matrix products, compute_tile(): jnp.einsum('hgqk,khd->hgqd', weights.astype(jnp.bfloat16), value_part, pr...  13.7 us
    dynamic_slice x16, local copies, waits for them, and re-layouts, one_key_block(): live_table[block_local, key_seq]  10.8 us
    dynamic_slice x16, local copies, waits for them, and re-layouts, one_key_block(): key_seq = block_order[offset // BLOCK_TOKENS]  9.25 us
  transfers between devices with their start and end apart: 8, of which 4 were waited for; matrix products, arithmetic and copies ran while one was open for 5% of the time, Pallas kernels for 0%

profile of v1, /device:TPU:0, one launch (start us, length us, event | category | flops | bytes accessed | tf_op | source)
XLA Modules:
  0.0 209.1 jit_solution(9342380660541550558)
XLA Ops:
  9.9 6.1 %collective-permute-start.1 = (bf16[256,256]{0,1:T(8,128)(2,1)S(1)}, bf16[256,256]{0,1:T(8,128)(2,1)S(1)}, u32[]{:S(2)}, u32[]{:S(2)}) collective-permute-start(bf16[256,256]{0,1:T(8,128)(2,1)S(1)} %copy.44), channel_id=1, source_target_pairs={{0,14},{2,0},{4,2},{6,4},{8,6},{10,8},{12,10},{14,12},{1,15},{3,1}... | collective-permute-start | bytes 393224 | tf_op jit(solution)/shard_map/ppermute | solution.py:30
  21.6 4.7 %collective-permute-start.3 = (bf16[256,256]{0,1:T(8,128)(2,1)S(1)}, bf16[256,256]{0,1:T(8,128)(2,1)S(1)}, u32[]{:S(2)}, u32[]{:S(2)}) collective-permute-start(bf16[256,256]{0,1:T(8,128)(2,1)S(1)} %collective-permute-done.1), channel_id=1, source_target_pairs={{0,14},{2,0},{4,2},{6,4},{8,6},{10,8},{12,10},{14,12},{1,15},{3,1}... | collective-permute-start | bytes 393224 | tf_op jit(solution)/shard_map/ppermute | solution.py:30
  27.6 2.3 %collective-permute-done.3 = bf16[256,256]{0,1:T(8,128)(2,1)S(1)} collective-permute-done((bf16[256,256]{0,1:T(8,128)(2,1)S(1)}, bf16[256,256]{0,1:T(8,128)(2,1)S(1)}, u32[]{:S(2)}, u32[]{:S(2)}) %collective-permute-start.3) | collective-permute-done | bytes 131104 | tf_op jit(solution)/shard_map/ppermute | solution.py:30
  29.9 5.4 %collective-permute-start.5 = (bf16[256,256]{0,1:T(8,128)(2,1)S(1)}, bf16[256,256]{0,1:T(8,128)(2,1)S(1)}, u32[]{:S(2)}, u32[]{:S(2)}) collective-permute-start(bf16[256,256]{0,1:T(8,128)(2,1)S(1)} %collective-permute-done.3), channel_id=1, source_target_pairs={{0,14},{2,0},{4,2},{6,4},{8,6},{10,8},{12,10},{14,12},{1,15},{3,1}... | collective-permute-start | bytes 393224 | tf_op jit(solution)/shard_map/ppermute | solution.py:30
  36.6 6.3 %collective-permute-done.4 = bf16[256,256]{0,1:T(8,128)(2,1)S(1)} collective-permute-done((bf16[256,256]{0,1:T(8,128)(2,1)S(1)}, bf16[256,256]{0,1:T(8,128)(2,1)S(1)}, u32[]{:S(2)}, u32[]{:S(2)}) %collective-permute-start.4) | collective-permute-done | bytes 131104 | tf_op jit(solution)/shard_map/ppermute | solution.py:23
  44.3 9.0 %collective-permute-done.6 = bf16[256,256]{0,1:T(8,128)(2,1)S(1)} collective-permute-done((bf16[256,256]{0,1:T(8,128)(2,1)S(1)}, bf16[256,256]{0,1:T(8,128)(2,1)S(1)}, u32[]{:S(2)}, u32[]{:S(2)}) %collective-permute-start.6) | collective-permute-done | bytes 131104 | tf_op jit(solution)/shard_map/ppermute | solution.py:23
  53.9 4.2 %all-gather.2.cloned.1.call-done = bf16[2048,256]{0,1:T(8,128)(2,1)} async-done(((bf16[256,256]{0,1:T(8,128)(2,1)}), bf16[2048,256]{0,1:T(8,128)(2,1)}) %all-gather.2.cloned.1.call-update) | async-done | bytes 1048592 | tf_op jit(solution)/shard_map/all_gather | solution.py:63
  58.8 134.3 %while.27 = (s32[]{:T(128)}, f32[2,8,128]{2,1,0:T(8,128)S(1)}, f32[2,8,128]{2,1,0:T(8,128)S(1)}, f32[2,8,128,128]{3,2,1,0:T(8,128)S(1)}, f32[2,8,128]{2,1,0:T(8,...) while((s32[]{:T(128)}, f32[2,8,128]{2,1,0:T(8,128)S(1)}, ...), condition=%wide.region_10.11_spmd.clone.clone, body=%wide.region_1.10_spmd.clone.clone.sunk | while | flops 274260000 | bytes 12501754 | solution.py:112
  63.9 1.9 conditional.8
  71.1 3.1 %conditional.9 = ((f32[2,8,128]{2,1,0:T(8,128)S(1)}, f32[2,8,128]{2,1,0:T(8,128)S(1)}, f32[2,8,128,128]{3,2,1,0:T(8,128)S(1)})) conditional(s32[]{:T(128)} %bitcast.60, (f32[2,8,128]{2,1,0:T(8,128)S(1)}, f32[2,8,128]{2,1,0:T(8,128)S(1)}, f32[2,8,128,128]{3,2,1,0:T(8,128)S(1)}) %tuple.96, (s32[2]{0:T(128)S(1)}, s32[]{:T(128)}, ...), branch_computations={%region_6.6_spmd, %region_7.9_spmd} | conditional | flops 137121792 | bytes 6111282 | solution.py:103
  81.3 3.1 %conditional.9 = ((f32[2,8,128]{2,1,0:T(8,128)S(1)}, f32[2,8,128]{2,1,0:T(8,128)S(1)}, f32[2,8,128,128]{3,2,1,0:T(8,128)S(1)})) conditional(s32[]{:T(128)} %bitcast.60, (f32[2,8,128]{2,1,0:T(8,128)S(1)}, f32[2,8,128]{2,1,0:T(8,128)S(1)}, f32[2,8,128,128]{3,2,1,0:T(8,128)S(1)}) %tuple.96, (s32[2]{0:T(128)S(1)}, s32[]{:T(128)}, ...), branch_computations={%region_6.6_spmd, %region_7.9_spmd} | conditional | flops 137121792 | bytes 6111282 | solution.py:103
  91.4 3.1 %conditional.9 = ((f32[2,8,128]{2,1,0:T(8,128)S(1)}, f32[2,8,128]{2,1,0:T(8,128)S(1)}, f32[2,8,128,128]{3,2,1,0:T(8,128)S(1)})) conditional(s32[]{:T(128)} %bitcast.60, (f32[2,8,128]{2,1,0:T(8,128)S(1)}, f32[2,8,128]{2,1,0:T(8,128)S(1)}, f32[2,8,128,128]{3,2,1,0:T(8,128)S(1)}) %tuple.96, (s32[2]{0:T(128)S(1)}, s32[]{:T(128)}, ...), branch_computations={%region_6.6_spmd, %region_7.9_spmd} | conditional | flops 137121792 | bytes 6111282 | solution.py:103
  99.7 1.9 conditional.8
  101.6 3.1 %conditional.9 = ((f32[2,8,128]{2,1,0:T(8,128)S(1)}, f32[2,8,128]{2,1,0:T(8,128)S(1)}, f32[2,8,128,128]{3,2,1,0:T(8,128)S(1)})) conditional(s32[]{:T(128)} %bitcast.60, (f32[2,8,128]{2,1,0:T(8,128)S(1)}, f32[2,8,128]{2,1,0:T(8,128)S(1)}, f32[2,8,128,128]{3,2,1,0:T(8,128)S(1)}) %tuple.96, (s32[2]{0:T(128)S(1)}, s32[]{:T(128)}, ...), branch_computations={%region_6.6_spmd, %region_7.9_spmd} | conditional | flops 137121792 | bytes 6111282 | solution.py:103
  109.9 1.9 conditional.8
  111.8 3.1 %conditional.9 = ((f32[2,8,128]{2,1,0:T(8,128)S(1)}, f32[2,8,128]{2,1,0:T(8,128)S(1)}, f32[2,8,128,128]{3,2,1,0:T(8,128)S(1)})) conditional(s32[]{:T(128)} %bitcast.60, (f32[2,8,128]{2,1,0:T(8,128)S(1)}, f32[2,8,128]{2,1,0:T(8,128)S(1)}, f32[2,8,128,128]{3,2,1,0:T(8,128)S(1)}) %tuple.96, (s32[2]{0:T(128)S(1)}, s32[]{:T(128)}, ...), branch_computations={%region_6.6_spmd, %region_7.9_spmd} | conditional | flops 137121792 | bytes 6111282 | solution.py:103
  125.3 3.1 %conditional.9 = ((f32[2,8,128]{2,1,0:T(8,128)S(1)}, f32[2,8,128]{2,1,0:T(8,128)S(1)}, f32[2,8,128,128]{3,2,1,0:T(8,128)S(1)})) conditional(s32[]{:T(128)} %bitcast.60, (f32[2,8,128]{2,1,0:T(8,128)S(1)}, f32[2,8,128]{2,1,0:T(8,128)S(1)}, f32[2,8,128,128]{3,2,1,0:T(8,128)S(1)}) %tuple.96, (s32[2]{0:T(128)S(1)}, s32[]{:T(128)}, ...), branch_computations={%region_6.6_spmd, %region_7.9_spmd} | conditional | flops 137121792 | bytes 6111282 | solution.py:103
  133.6 3.1 %conditional.9 = ((f32[2,8,128]{2,1,0:T(8,128)S(1)}, f32[2,8,128]{2,1,0:T(8,128)S(1)}, f32[2,8,128,128]{3,2,1,0:T(8,128)S(1)})) conditional(s32[]{:T(128)} %bitcast.60, (f32[2,8,128]{2,1,0:T(8,128)S(1)}, f32[2,8,128]{2,1,0:T(8,128)S(1)}, f32[2,8,128,128]{3,2,1,0:T(8,128)S(1)}) %tuple.96, (s32[2]{0:T(128)S(1)}, s32[]{:T(128)}, ...), branch_computations={%region_6.6_spmd, %region_7.9_spmd} | conditional | flops 137121792 | bytes 6111282 | solution.py:103
  143.8 3.1 %conditional.9 = ((f32[2,8,128]{2,1,0:T(8,128)S(1)}, f32[2,8,128]{2,1,0:T(8,128)S(1)}, f32[2,8,128,128]{3,2,1,0:T(8,128)S(1)})) conditional(s32[]{:T(128)} %bitcast.60, (f32[2,8,128]{2,1,0:T(8,128)S(1)}, f32[2,8,128]{2,1,0:T(8,128)S(1)}, f32[2,8,128,128]{3,2,1,0:T(8,128)S(1)}) %tuple.96, (s32[2]{0:T(128)S(1)}, s32[]{:T(128)}, ...), branch_computations={%region_6.6_spmd, %region_7.9_spmd} | conditional | flops 137121792 | bytes 6111282 | solution.py:103
  152.0 1.9 conditional.8
  154.0 3.1 %conditional.9 = ((f32[2,8,128]{2,1,0:T(8,128)S(1)}, f32[2,8,128]{2,1,0:T(8,128)S(1)}, f32[2,8,128,128]{3,2,1,0:T(8,128)S(1)})) conditional(s32[]{:T(128)} %bitcast.60, (f32[2,8,128]{2,1,0:T(8,128)S(1)}, f32[2,8,128]{2,1,0:T(8,128)S(1)}, f32[2,8,128,128]{3,2,1,0:T(8,128)S(1)}) %tuple.96, (s32[2]{0:T(128)S(1)}, s32[]{:T(128)}, ...), branch_computations={%region_6.6_spmd, %region_7.9_spmd} | conditional | flops 137121792 | bytes 6111282 | solution.py:103
  167.5 3.1 %conditional.9 = ((f32[2,8,128]{2,1,0:T(8,128)S(1)}, f32[2,8,128]{2,1,0:T(8,128)S(1)}, f32[2,8,128,128]{3,2,1,0:T(8,128)S(1)})) conditional(s32[]{:T(128)} %bitcast.60, (f32[2,8,128]{2,1,0:T(8,128)S(1)}, f32[2,8,128]{2,1,0:T(8,128)S(1)}, f32[2,8,128,128]{3,2,1,0:T(8,128)S(1)}) %tuple.96, (s32[2]{0:T(128)S(1)}, s32[]{:T(128)}, ...), branch_computations={%region_6.6_spmd, %region_7.9_spmd} | conditional | flops 137121792 | bytes 6111282 | solution.py:103
  190.0 3.1 %conditional.9 = ((f32[2,8,128]{2,1,0:T(8,128)S(1)}, f32[2,8,128]{2,1,0:T(8,128)S(1)}, f32[2,8,128,128]{3,2,1,0:T(8,128)S(1)})) conditional(s32[]{:T(128)} %bitcast.60, (f32[2,8,128]{2,1,0:T(8,128)S(1)}, f32[2,8,128]{2,1,0:T(8,128)S(1)}, f32[2,8,128,128]{3,2,1,0:T(8,128)S(1)}) %tuple.96, (s32[2]{0:T(128)S(1)}, s32[]{:T(128)}, ...), branch_computations={%region_6.6_spmd, %region_7.9_spmd} | conditional | flops 137121792 | bytes 6111282 | solution.py:103
  195.1 4.6 %all_to_all.16 = bf16[2,128,2048]{2,1,0:T(8,128)(2,1)S(1)} all-to-all(bf16[2,128,2048]{2,1,0:T(8,128)(2,1)S(1)} %convert_element_type.44), channel_id=1, replica_groups=mesh['rep'=2,'ctx'=8,'tp'=2] {'tp'}, dimensions={0} | all-to-all | bytes 2097152 | tf_op jit(solution)/shard_map/all_to_all | solution.py:123
  (278 shorter events, 94.0 us)
Async XLA Ops:
  7.2 9.6 %copy-start = (s32[16,12]{1,0:T(8,128)S(1)}, s32[16,12]{1,0:T(8,128)}, u32[]{:S(2)}) copy-start(s32[16,12]{1,0:T(8,128)} %param.15) | copy-start | bytes 2308
  7.2 51.0 %all-gather.2.cloned.1.call-start = ((), (), s32[]{:S(2)}) async-start(), calls=%async_computation.1 | async-start | bytes 1179648 | tf_op jit(solution)/shard_map/all_gather | solution.py:63
  9.9 11.7 %collective-permute-start.1 = (bf16[256,256]{0,1:T(8,128)(2,1)S(1)}, bf16[256,256]{0,1:T(8,128)(2,1)S(1)}, u32[]{:S(2)}, u32[]{:S(2)}) collective-permute-start(bf16[256,256]{0,1:T(8,128)(2,1)S(1)} %copy.44), channel_id=1, source_target_pairs={{0,14},{2,0},{4,2},{6,4},{8,6},{10,8},{12,10},{14,12},{1,15},{3,1}... | collective-permute-start | bytes 393224 | tf_op jit(solution)/shard_map/ppermute | solution.py:30
  16.0 10.3 %collective-permute-start = (bf16[256,256]{0,1:T(8,128)(2,1)S(1)}, bf16[256,256]{0,1:T(8,128)(2,1)S(1)}, u32[]{:S(2)}, u32[]{:S(2)}) collective-permute-start(bf16[256,256]{0,1:T(8,128)(2,1)S(1)} %copy.44), channel_id=1, source_target_pairs={{0,2},{2,4},{4,6},{6,8},{8,10},{10,12},{12,14},{14,0},{1,3},{3,5},... | collective-permute-start | bytes 393224 | tf_op jit(solution)/shard_map/ppermute | solution.py:23
  21.6 8.3 %collective-permute-start.3 = (bf16[256,256]{0,1:T(8,128)(2,1)S(1)}, bf16[256,256]{0,1:T(8,128)(2,1)S(1)}, u32[]{:S(2)}, u32[]{:S(2)}) collective-permute-start(bf16[256,256]{0,1:T(8,128)(2,1)S(1)} %collective-permute-done.1), channel_id=1, source_target_pairs={{0,14},{2,0},{4,2},{6,4},{8,6},{10,8},{12,10},{14,12},{1,15},{3,1}... | collective-permute-start | bytes 393224 | tf_op jit(solution)/shard_map/ppermute | solution.py:30
  26.3 9.0 %collective-permute-start.2 = (bf16[256,256]{0,1:T(8,128)(2,1)S(1)}, bf16[256,256]{0,1:T(8,128)(2,1)S(1)}, u32[]{:S(2)}, u32[]{:S(2)}) collective-permute-start(bf16[256,256]{0,1:T(8,128)(2,1)S(1)} %collective-permute-done), channel_id=1, source_target_pairs={{0,2},{2,4},{4,6},{6,8},{8,10},{10,12},{12,14},{14,0},{1,3},{3,5},... | collective-permute-start | bytes 393224 | tf_op jit(solution)/shard_map/ppermute | solution.py:23
  29.9 13.7 %collective-permute-start.5 = (bf16[256,256]{0,1:T(8,128)(2,1)S(1)}, bf16[256,256]{0,1:T(8,128)(2,1)S(1)}, u32[]{:S(2)}, u32[]{:S(2)}) collective-permute-start(bf16[256,256]{0,1:T(8,128)(2,1)S(1)} %collective-permute-done.3), channel_id=1, source_target_pairs={{0,14},{2,0},{4,2},{6,4},{8,6},{10,8},{12,10},{14,12},{1,15},{3,1}... | collective-permute-start | bytes 393224 | tf_op jit(solution)/shard_map/ppermute | solution.py:30
  35.3 7.7 %collective-permute-start.4 = (bf16[256,256]{0,1:T(8,128)(2,1)S(1)}, bf16[256,256]{0,1:T(8,128)(2,1)S(1)}, u32[]{:S(2)}, u32[]{:S(2)}) collective-permute-start(bf16[256,256]{0,1:T(8,128)(2,1)S(1)} %collective-permute-done.2), channel_id=1, source_target_pairs={{0,2},{2,4},{4,6},{6,8},{8,10},{10,12},{12,14},{14,0},{1,3},{3,5},... | collective-permute-start | bytes 393224 | tf_op jit(solution)/shard_map/ppermute | solution.py:23
  42.9 10.3 %collective-permute-start.6 = (bf16[256,256]{0,1:T(8,128)(2,1)S(1)}, bf16[256,256]{0,1:T(8,128)(2,1)S(1)}, u32[]{:S(2)}, u32[]{:S(2)}) collective-permute-start(bf16[256,256]{0,1:T(8,128)(2,1)S(1)} %collective-permute-done.4), channel_id=1, source_target_pairs={{0,2},{2,4},{4,6},{6,8},{8,10},{10,12},{12,14},{14,0},{1,3},{3,5},... | collective-permute-start | bytes 393224 | tf_op jit(solution)/shard_map/ppermute | solution.py:23
  58.1 0.7 copy-start.1
Sparse Core Ops, SparseCore 0:
  10.0 48.0 all-gather.1
